TPU v7x, 128 devices: a whole 4x4x4 slice. The times are simulated.
128 devices in a mesh: frames: 2 (over y_hi), codebook: 16 (over y_lo, x, core), hidden: 4 (over z).
Axes of the slice: x: 4, y: 4 (y_hi: 2, y_lo: 2; y = y_hi * 2 + y_lo), z: 4, core: 2. Of those that a mesh axis runs over, the one named last changes fastest.
Arguments:
- temporal: bfloat16 [4096, 4096], P(('frames', 'codebook'), 'hidden'), may hold values from -6 to 6
- frame_ids: int32 [4096, 16], P('frames', 'codebook'), may hold values from 0 to 2047
- proj_weight: bfloat16 [16, 4096, 1024], P('codebook', 'hidden'), may hold values from -0.09375 to 0.09375
- embed_table: bfloat16 [16, 2049, 1024], P('codebook'), may hold values from -6 to 6
- qkv_weight: bfloat16 [16, 3, 1024, 1024], P('codebook', None, None, 'hidden'), may hold values from -12 to 12
- out_weight: bfloat16 [16, 1024, 1024], P('codebook', 'hidden'), may hold values from -0.1875 to 0.1875
- gate_up: bfloat16 [16, 2, 1024, 4096], P('codebook', None, None, 'hidden'), may hold values from -0.1875 to 0.1875
- down_weight: bfloat16 [16, 4096, 1024], P('codebook', 'hidden'), may hold values from -0.09375 to 0.09375
- norm_gains: float32 [16, 2, 1024], P('codebook'), may hold values from 0.25 to 1.75
Outputs:
- depth_states: float32 [16, 4096, 1024], P('codebook', 'frames', 'hidden')
All inputs are finite; a program needn't handle non-finite values.
Results may differ from a plain program's by a relative error of at most 0.015.
Values may be sent and summed in bfloat16 or wider, within the bound.
A program may use at most 192 MiB of HBM per device.

v0:
```python
import jax
import jax.numpy as jnp
from jax import lax
from jax.sharding import PartitionSpec as P

HEADS = 16


def shifted(block, axis, distance):
    devices = range(lax.axis_size(axis))
    route = [(i - distance, i) for i in devices if i - distance in devices]
    return lax.ppermute(block, axis, route)


def normalize(values, norm_gain):
    return values * lax.rsqrt(jnp.mean(values * values, axis=-1, keepdims=True) + 1e-05) * norm_gain


def gated(normed, piece):
    gate_sum = jnp.dot(normed, piece[0], preferred_element_type=jnp.float32)
    upper_sum = jnp.dot(normed, piece[1], preferred_element_type=jnp.float32)
    return (jax.nn.silu(gate_sum) * upper_sum).astype(jnp.bfloat16)


def body(
    temporal,
    frame_ids,
    proj_weight,
    embed_table,
    qkv_weight,
    out_weight,
    gate_up,
    down_weight,
    norm_gains,
):
    code_index = lax.axis_index("codebook")
    hidden_index = lax.axis_index("hidden")
    hidden_count = lax.axis_size("hidden")
    start_id = embed_table.shape[1] - 1
    token_table = embed_table[0]
    norm_gain = norm_gains[0]
    earlier = shifted(frame_ids, "codebook", 1)[:, 0]
    previous = jnp.where(code_index == 0, start_id, earlier)
    partial_sum = jnp.dot(
        lax.all_gather(temporal, "codebook", axis=0, tiled=True),
        proj_weight[0],
        preferred_element_type=jnp.float32,
    )
    row_count = partial_sum.shape[0]
    x_zero = lax.psum(partial_sum.astype(jnp.bfloat16), "hidden").astype(jnp.float32) + token_table[
        previous
    ].astype(jnp.float32)
    normed = normalize(x_zero, norm_gain[0]).astype(jnp.bfloat16)
    local_width = qkv_weight.shape[3]
    local_heads = HEADS // hidden_count
    head_size = local_width // local_heads
    triple = jnp.einsum(
        "rd,kdc->krc", normed, qkv_weight[0], preferred_element_type=jnp.float32
    ).astype(jnp.bfloat16)
    query_heads = triple[0].reshape(row_count, local_heads, head_size)
    highest = jnp.full((row_count, local_heads), -1e30, jnp.float32)
    key_piece = lax.all_gather(triple[1][None], "codebook", axis=0, tiled=True)
    value_piece = lax.all_gather(triple[2][None], "codebook", axis=0, tiled=True)
    positions = key_piece.shape[0]
    key_heads = key_piece.reshape(positions, row_count, local_heads, head_size)
    value_heads = value_piece.reshape(positions, row_count, local_heads, head_size)
    scores = jnp.einsum(
        "fhd,jfhd->jfh", query_heads, key_heads, preferred_element_type=jnp.float32
    ) * head_size ** (-0.5)
    valid = (jnp.arange(positions, dtype=jnp.int32) <= code_index)[:, None, None]
    scores = jnp.where(valid, scores, -1e30)
    new_highest = jnp.maximum(highest, jnp.max(scores, axis=0))
    weights = jnp.where(valid, jnp.exp(scores - new_highest[None]), 0.0)
    running = jnp.sum(weights, axis=0)
    summed = jnp.einsum(
        "jfh,jfhd->fhd",
        weights.astype(jnp.bfloat16),
        value_heads,
        preferred_element_type=jnp.float32,
    )
    highest, running, summed = (new_highest, running, summed)
    attended = (summed / running[..., None]).reshape(row_count, local_width).astype(jnp.bfloat16)
    attention_part = jnp.dot(attended, out_weight[0], preferred_element_type=jnp.float32)
    residual = x_zero + lax.psum(attention_part.astype(jnp.bfloat16), "hidden").astype(jnp.float32)
    normed_two = normalize(residual, norm_gain[1]).astype(jnp.bfloat16)
    activated = gated(normed_two, gate_up[0])
    down_part = jnp.dot(activated, down_weight[0], preferred_element_type=jnp.float32)
    mlp_piece = lax.psum_scatter(
        down_part.astype(jnp.bfloat16), "hidden", scatter_dimension=1, tiled=True
    ).astype(jnp.float32)
    own_residual = lax.dynamic_slice_in_dim(residual, hidden_index * local_width, local_width, 1)
    return (own_residual + mlp_piece)[None]


def solution(mesh):
    placed = (
        P(("frames", "codebook"), "hidden"),
        P("frames", "codebook"),
        P("codebook", "hidden", None),
        P("codebook", None, None),
        P("codebook", None, None, "hidden"),
        P("codebook", "hidden", None),
        P("codebook", None, None, "hidden"),
        P("codebook", "hidden", None),
        P("codebook", None, None),
    )
    return jax.shard_map(
        body,
        mesh=mesh,
        in_specs=placed,
        out_specs=P("codebook", "frames", "hidden"),
        check_vma=False,
    )
```

profile of v0, /device:TPU:1, one launch (start us, length us, event | category | flops | bytes accessed | tf_op | source)
XLA Modules:
  0.0 563.1 jit_solution(17674491881883395552)
XLA Ops:
  6.5 0.7 all-gather.4.cloned.1.call-update
  7.3 42.5 %all-gather.4.cloned.1.call-done = bf16[2048,1024]{1,0:T(8,128)(2,1)} async-done(((bf16[128,1024]{1,0:T(8,128)(2,1)}), bf16[2048,1024]{1,0:T(8,128)(2,1)}) %all-gather.4.cloned.1.call-update) | async-done | bytes 4194320 | tf_op jit(solution)/shard_map/all_gather | solution.py:45
  49.8 8.3 %convolution_convert_fusion.2 = bf16[2048,1024]{1,0:T(8,128)(2,1)} fusion(bf16[2048,1024]{1,0:T(8,128)(2,1)} %all-gather.4.cloned.1.call-done, bf16[1,1024,1024]{2,1,0:T(8,128)(2,1)S(1)} %copy-done), kind=kOutput, calls=%fused_computation.16 | convolution fusion | flops 4297064448 | bytes 10485760 | tf_op jit(solution)/shard_map/dot_general | solution.py:44
  58.2 0.6 copy-done.9
  58.9 2.8 collective-permute-start
  61.8 0.7 collective-permute-done
  62.5 13.8 %gather_fusion = bf16[2048,1024]{1,0:T(8,128)(2,1)} fusion(bf16[2049,1024]{1,0:T(8,128)(2,1)} %bitcast.66, s32[2048]{0:T(1024)S(1)} %broadcast_clamp_fusion), kind=kCustom, calls=%fused_computation | custom fusion | bytes 8396800 | tf_op jit(solution)/shard_map/gather | solution.py:50
  76.3 74.6 %all-reduce.3.cloned.1.call-done = bf16[2048,1024]{1,0:T(8,128)(2,1)} async-done(((bf16[2048,1024]{1,0:T(8,128)(2,1)}), bf16[2048,1024]{1,0:T(8,128)(2,1)}) %all-reduce.3.cloned.1.call-update) | async-done | bytes 4194320 | tf_op jit(solution)/shard_map/psum | solution.py:50
  150.9 5.0 multiply_reduce_fusion.3
  156.0 0.9 copy-done.3
  156.8 4.2 fusion.8
  161.0 0.3 fusion.30
  161.3 1.3 copy.21
  162.7 1.3 copy.23
  164.3 0.2 convert.1
  164.6 90.1 %all-gather.6.cloned.1.call-done = bf16[16,2048,256]{2,1,0:T(8,128)(2,1)} async-done(((bf16[1,2048,256]{2,1,0:T(8,128)(2,1)}), bf16[16,2048,256]{2,1,0:T(8,128)(2,1)}) %all-gather.6.cloned.1.call-update) | async-done | bytes 16777232 | tf_op jit(solution)/shard_map/all_gather | solution.py:62
  254.7 22.0 %copy.40 = bf16[16,2048,256]{1,2,0:T(8,128)(2,1)} copy(bf16[16,2048,256]{2,1,0:T(8,128)(2,1)} %all-gather.6.cloned.1.call-done) | data formatting | bytes 33554432
  276.7 7.9 %multiply_reduce_fusion.1 = f32[2048,4,16]{0,1,2:T(4,128)S(1)} fusion(f32[2048,4,64]{0,2,1:T(8,128)S(1)} %convert.1, bf16[16,2048,256]{1,2,0:T(8,128)(2,1)} %copy.40), kind=kLoop, calls=%fused_computation.2 | loop fusion | flops 25034752 | bytes 19398656
  284.5 0.4 bitcast_reduce_fusion
  284.9 0.5 fusion.25
  285.4 0.3 copy.43
  285.8 62.8 %all-gather.8.cloned.1.call-done = bf16[16,2048,256]{2,1,0:T(8,128)(2,1)} async-done(((bf16[1,2048,256]{2,1,0:T(8,128)(2,1)}), bf16[16,2048,256]{2,1,0:T(8,128)(2,1)}) %all-gather.8.cloned.1.call-update) | async-done | bytes 16777232 | tf_op jit(solution)/shard_map/all_gather | solution.py:63
  348.6 21.7 %copy.41 = bf16[16,2048,256]{1,2,0:T(8,128)(2,1)} copy(bf16[16,2048,256]{2,1,0:T(8,128)(2,1)} %all-gather.8.cloned.1.call-done) | data formatting | bytes 33554432
  370.3 7.7 %multiply_reduce_fusion = f32[2048,4,64]{0,2,1:T(8,128)S(1)} fusion(bf16[2048,4,16,64]{0,3,1,2:T(8,128)(2,1)} %bitcast.67, f32[2048,4,16]{0,1,2:T(4,128)S(1)} %copy.43), kind=kLoop, calls=%fused_computation.1 | loop fusion | flops 24641536 | bytes 19398656 | tf_op jit(solution)/shard_map/jfh,jfhd->fhd/dot_general | solution.py:75
  378.1 3.3 convolution_convert_fusion
  381.5 93.4 %all-reduce.5.cloned.1.call-done = bf16[2048,1024]{1,0:T(8,128)(2,1)} async-done(((bf16[2048,1024]{1,0:T(8,128)(2,1)}), bf16[2048,1024]{1,0:T(8,128)(2,1)}) %all-reduce.5.cloned.1.call-update) | async-done | bytes 4194320 | tf_op jit(solution)/shard_map/psum | solution.py:84
  474.9 5.8 %multiply_reduce_fusion.2 = (f32[2048]{0:T(1024)S(1)}, f32[2048,1024]{1,0:T(8,128)S(1)}) fusion(bf16[2048,1024]{1,0:T(8,128)(2,1)} %all-reduce.5.cloned.1.call-done, bf16[2048,1024]{1,0:T(8,128)(2,1)} %gather_fusion, bf16[2048,1024]{1,0:T(8,128)(2,1)} %all-reduce.3.cloned.1.call-done), kind=kLoop, calls=%fused_computation.5 | loop fusion | flops 14678016 | bytes 20979712 | tf_op jit(solution)/shard_map/reduce_sum | solution.py:16
  480.7 3.2 copy-done.4
  483.9 6.7 %fusion.14 = f32[2048,1024]{1,0:T(8,128)} fusion(bf16[1,2,1024,1024]{3,2,1,0:T(8,128)(2,1)S(1)} %copy-done.7, f32[2048,1024]{1,0:T(8,128)S(1)} %get-tuple-element.6, f32[1024]{0:T(1024)S(1)} %bitcast.71, f32[2048]{0:T(1024)S(1)} %add_rsqrt_fusion), kind=kOutput, calls=%fused_computation.21 | convolution fusion | flops 4301258752 | bytes 18886656 | tf_op jit(solution)/shard_map/dot_general | solution.py:20
  490.6 15.1 %convolution_convert_fusion.1 = bf16[2048,1024]{1,0:T(8,128)(2,1)} fusion(f32[2048,1024]{1,0:T(8,128)} %fusion.14, bf16[1,1024,1024]{2,1,0:T(8,128)(2,1)} %param.16, bf16[1,2,1024,1024]{3,2,1,0:T(8,128)(2,1)} %param.15, f32[2048,1024]{1,0:T(8,128)} %copy-done.4, f32[1024]{0:T(1024)S(1)} %bitcast.72, f32[2048]{0:T(1024)S(1)} %add_rsqrt_fusion), kind=kOutput, calls=%fused_computation.15 | convolution fusion | flops 8610906112 | bytes 25178112 | tf_op jit(solution)/shard_map/dot_general | solution.py:87
  505.8 47.0 %reduce-scatter.2.cloned.1.call-done = bf16[2048,256]{1,0:T(8,128)(2,1)} async-done(((bf16[2048,1024]{1,0:T(8,128)(2,1)}), bf16[2048,256]{1,0:T(8,128)(2,1)}) %reduce-scatter.2.cloned.1.call-update) | async-done | bytes 1048592 | tf_op jit(solution)/shard_map/reduce_scatter | solution.py:88
  552.9 3.4 add_bitcast_fusion
  (36 shorter events, 0.8 us)
Async XLA Ops:
  6.5 43.3 %copy-start = (bf16[1,1024,1024]{2,1,0:T(8,128)(2,1)S(1)}, bf16[1,1024,1024]{2,1,0:T(8,128)(2,1)}, u32[]{:S(2)}) copy-start(bf16[1,1024,1024]{2,1,0:T(8,128)(2,1)} %param.11) | copy-start | bytes 6291460
  6.5 43.3 %all-gather.4.cloned.1.call-start = ((), (), s32[]{:S(2)}) async-start(), calls=%async_computation.1 | async-start | bytes 4456448 | tf_op jit(solution)/shard_map/all_gather | solution.py:45
  7.3 143.6 %all-reduce.3.cloned.1.call-start = ((), (), s32[]{:S(2)}) async-start(), calls=%async_computation.2 | async-start | bytes 8388608 | tf_op jit(solution)/shard_map/psum | solution.py:50
  58.2 0.7 copy-start.9
  58.2 3.5 copy-start.6
  58.2 196.5 %all-gather.6.cloned.1.call-start = ((), (), s32[]{:S(2)}) async-start(), calls=%async_computation.3 | async-start | bytes 17825792 | tf_op jit(solution)/shard_map/all_gather | solution.py:62
  58.9 3.6 collective-permute-start
  62.5 93.4 %copy-start.8 = (bf16[1,3,1024,256]{3,2,1,0:T(8,128)(2,1)S(1)}, bf16[1,3,1024,256]{3,2,1,0:T(8,128)(2,1)}, u32[]{:S(2)}) copy-start(bf16[1,3,1024,256]{3,2,1,0:T(8,128)(2,1)} %param.13) | copy-start | bytes 4718596
  150.9 5.1 copy-start.2
  150.9 5.9 %copy-start.3 = (bf16[2048,1024]{1,0:T(8,128)(2,1)S(1)}, bf16[2048,1024]{1,0:T(8,128)(2,1)}, u32[]{:S(2)}) copy-start(bf16[2048,1024]{1,0:T(8,128)(2,1)} %all-reduce.3.cloned.1.call-done) | copy-start | bytes 12582916
  162.7 185.9 %all-gather.8.cloned.1.call-start = ((), (), s32[]{:S(2)}) async-start(), calls=%async_computation.4 | async-start | bytes 17825792 | tf_op jit(solution)/shard_map/all_gather | solution.py:63
  164.1 310.8 %all-reduce.5.cloned.1.call-start = ((), (), s32[]{:S(2)}) async-start(), calls=%async_computation.5 | async-start | bytes 8388608 | tf_op jit(solution)/shard_map/psum | solution.py:84
  370.3 7.9 %copy-start.5 = (bf16[1,256,1024]{2,1,0:T(8,128)(2,1)S(1)}, bf16[1,256,1024]{2,1,0:T(8,128)(2,1)}, u32[]{:S(2)}) copy-start(bf16[1,256,1024]{2,1,0:T(8,128)(2,1)} %param.14) | copy-start | bytes 1572868
  381.4 171.4 %reduce-scatter.2.cloned.1.call-start = ((), (), s32[]{:S(2)}) async-start(), calls=%async_computation.6 | async-start | bytes 5242880 | tf_op jit(solution)/shard_map/reduce_scatter | solution.py:88
  474.9 9.1 %copy-start.7 = (bf16[1,2,1024,1024]{3,2,1,0:T(8,128)(2,1)S(1)}, bf16[1,2,1024,1024]{3,2,1,0:T(8,128)(2,1)}, u32[]{:S(2)}) copy-start(bf16[1,2,1024,1024]{3,2,1,0:T(8,128)(2,1)} %param.15) | copy-start | bytes 12582916
  480.7 3.2 copy-start.4
  505.8 50.5 %copy-start.1 = (bf16[1,1024,1024]{2,1,0:T(8,128)(2,1)S(1)}, bf16[1,1024,1024]{2,1,0:T(8,128)(2,1)}, u32[]{:S(2)}) copy-start(bf16[1,1024,1024]{2,1,0:T(8,128)(2,1)} %param.11) | copy-start | bytes 6291460
Sparse Core Ops, SparseCore 0:
  9.0 40.7 all-gather.3
  58.3 92.5 all-reduce.2
  162.8 91.8 all-gather.5
  256.2 92.3 all-gather.7
  381.6 93.2 all-reduce.4
  505.9 46.8 reduce-scatter.1
where the time goes:
time: 564 us; the launch traced here: 563 us
  waiting for transfers between devices  412 us (73%)
  local copies, waits for them, and re-layouts  65.5 us (12%)
  matrix products  37.6 us (7%)
  other arithmetic  31.1 us (6%)
  between operations  13.7 us (2%)
    psum x1, waiting for transfers between devices, body(): lax.psum(attention_part.astype(jnp.bfloat16), 'hidden').astype(jnp.float32)  93.4 us
    all_gather x1, waiting for transfers between devices, body(): key_piece = lax.all_gather(triple[1][None], 'codebook', axis=0, tiled=True)  90.1 us
    psum x1, waiting for transfers between devices, body(): lax.psum(partial_sum.astype(jnp.bfloat16), 'hidden').astype(jnp.float32)  74.6 us
    all_gather x1, waiting for transfers between devices, body(): lax.all_gather(triple[2][None], 'codebook', axis=0, tiled=True)  62.8 us
    unnamed x23, local copies, waits for them, and re-layouts  48.7 us
    reduce_scatter x1, waiting for transfers between devices, body(): lax.psum_scatter(down_part.astype(jnp.bfloat16), 'hidden', scatter_dimens...  47 us
    all_gather x1, waiting for transfers between devices, body(): lax.all_gather(temporal, 'codebook', axis=0, tiled=True)  42.5 us
    dot_general x1, matrix products, body(): jnp.dot(activated, down_weight[0], preferred_element_type=jnp.float32)  15.1 us
  transfers between devices with their start and end apart: 7, of which 7 were waited for; matrix products, arithmetic and copies ran while one was open for 8% of the time, Pallas kernels for 0%

commit v1 on v0

--- a/solution.py
+++ b/solution.py
@@ -42,7 +42,10 @@
     earlier = shifted(frame_ids, "codebook", 1)[:, 0]
     previous = jnp.where(code_index == 0, start_id, earlier)
     partial_sum = jnp.dot(
-        lax.all_gather(temporal, "codebook", axis=0, tiled=True),
+        jnp.concatenate(
+            lax.all_to_all(jnp.stack([temporal] * lax.axis_size("codebook")), "codebook", 0, 0),
+            axis=0,
+        ),
         proj_weight[0],
         preferred_element_type=jnp.float32,
     )

time: 564 us -> 576 us (1.021)
  blocking collectives: 0 us -> 55.4 us
  waiting for transfers between devices: 412 us -> 371 us
    all_to_all x0 -> x1, blocking collectives: none -> 55.4 us  [body(): lax.all_to_all(jnp.stack([temporal] * lax.axis_size('codebook')), 'codebo...]
    all_gather x1 -> x0, waiting for transfers between devices: 42.5 us -> none  [body(): lax.all_gather(temporal, 'codebook', axis=0, tiled=True)]
  transfers between devices with their start and end apart: 7 -> 6, of which waited for: 7 -> 6; matrix products, arithmetic and copies ran while one was open for 8% -> 8% of each run, Pallas kernels for 0% -> 0%
where the time goes in v1:
time: 576 us; the launch traced here: 575 us
  waiting for transfers between devices  371 us (64%)
  local copies, waits for them, and re-layouts  67.2 us (12%)
  blocking collectives  55.4 us (10%)
  matrix products  35.3 us (6%)
  other arithmetic  31.1 us (5%)
  between operations  13.3 us (2%)
    psum x1, waiting for transfers between devices, body(): lax.psum(attention_part.astype(jnp.bfloat16), 'hidden').astype(jnp.float32)  93.4 us
    all_gather x1, waiting for transfers between devices, body(): key_piece = lax.all_gather(triple[1][None], 'codebook', axis=0, tiled=True)  90.1 us
    psum x1, waiting for transfers between devices, body(): lax.psum(partial_sum.astype(jnp.bfloat16), 'hidden').astype(jnp.float32)  75.6 us
    all_gather x1, waiting for transfers between devices, body(): lax.all_gather(triple[2][None], 'codebook', axis=0, tiled=True)  62.9 us
    all_to_all x1, blocking collectives, body(): lax.all_to_all(jnp.stack([temporal] * lax.axis_size('codebook')), 'codebo...  55.4 us
    unnamed x23, local copies, waits for them, and re-layouts  48.8 us
    reduce_scatter x1, waiting for transfers between devices, body(): lax.psum_scatter(down_part.astype(jnp.bfloat16), 'hidden', scatter_dimens...  47 us
    dot_general x1, matrix products, body(): jnp.dot(activated, down_weight[0], preferred_element_type=jnp.float32)  15.1 us
  transfers between devices with their start and end apart: 6, of which 6 were waited for; matrix products, arithmetic and copies ran while one was open for 8% of the time, Pallas kernels for 0%

profile of v1, /device:TPU:1, one launch (start us, length us, event | category | flops | bytes accessed | tf_op | source)
XLA Modules:
  0.0 575.1 jit_solution(14632051651494889656)
XLA Ops:
  6.5 1.6 stack.2
  8.2 55.4 %all_to_all.5 = bf16[16,128,1024]{2,1,0:T(8,128)(2,1)S(1)} all-to-all(bf16[16,128,1024]{2,1,0:T(8,128)(2,1)S(1)} %stack.2), channel_id=1, replica_groups=mesh['frames'=2,'codebook'=16,'hidden'=4] {'codebook'}, dimensions={0} | all-to-all | bytes 8388608 | tf_op jit(solution)/shard_map/all_to_all | solution.py:46
  63.6 6.0 %convolution_convert_fusion.2 = bf16[2048,1024]{1,0:T(8,128)(2,1)} fusion(bf16[2048,1024]{1,0:T(8,128)(2,1)S(1)} %bitcast.70, bf16[1,1024,1024]{2,1,0:T(8,128)(2,1)S(1)} %copy-done), kind=kOutput, calls=%fused_computation.16 | convolution fusion | flops 4297064448 | bytes 10485760 | tf_op jit(solution)/shard_map/dot_general | solution.py:44
  69.7 0.6 copy-done.9
  70.3 1.9 collective-permute-start
  72.2 1.4 collective-permute-done
  73.7 13.8 %gather_fusion = bf16[2048,1024]{1,0:T(8,128)(2,1)} fusion(bf16[2049,1024]{1,0:T(8,128)(2,1)} %bitcast.67, s32[2048]{0:T(1024)S(1)} %broadcast_clamp_fusion), kind=kCustom, calls=%fused_computation | custom fusion | bytes 8396800 | tf_op jit(solution)/shard_map/gather | solution.py:53
  87.5 75.6 %all-reduce.3.cloned.1.call-done = bf16[2048,1024]{1,0:T(8,128)(2,1)} async-done(((bf16[2048,1024]{1,0:T(8,128)(2,1)}), bf16[2048,1024]{1,0:T(8,128)(2,1)}) %all-reduce.3.cloned.1.call-update) | async-done | bytes 4194320 | tf_op jit(solution)/shard_map/psum | solution.py:53
  163.1 5.0 multiply_reduce_fusion.3
  168.1 0.9 copy-done.3
  169.0 4.2 fusion.8
  173.2 0.3 fusion.30
  173.5 1.3 copy.21
  174.9 1.3 copy.23
  176.5 0.2 convert.1
  176.7 90.1 %all-gather.3.cloned.1.call-done = bf16[16,2048,256]{2,1,0:T(8,128)(2,1)} async-done(((bf16[1,2048,256]{2,1,0:T(8,128)(2,1)}), bf16[16,2048,256]{2,1,0:T(8,128)(2,1)}) %all-gather.3.cloned.1.call-update) | async-done | bytes 16777232 | tf_op jit(solution)/shard_map/all_gather | solution.py:65
  266.8 22.1 %copy.40 = bf16[16,2048,256]{1,2,0:T(8,128)(2,1)} copy(bf16[16,2048,256]{2,1,0:T(8,128)(2,1)} %all-gather.3.cloned.1.call-done) | data formatting | bytes 33554432
  288.9 7.9 %multiply_reduce_fusion.1 = f32[2048,4,16]{0,1,2:T(4,128)S(1)} fusion(f32[2048,4,64]{0,2,1:T(8,128)S(1)} %convert.1, bf16[16,2048,256]{1,2,0:T(8,128)(2,1)} %copy.40), kind=kLoop, calls=%fused_computation.2 | loop fusion | flops 25034752 | bytes 19398656
  296.7 0.4 bitcast_reduce_fusion
  297.1 0.5 fusion.25
  297.6 0.3 copy.43
  298.0 62.9 %all-gather.5.cloned.1.call-done = bf16[16,2048,256]{2,1,0:T(8,128)(2,1)} async-done(((bf16[1,2048,256]{2,1,0:T(8,128)(2,1)}), bf16[16,2048,256]{2,1,0:T(8,128)(2,1)}) %all-gather.5.cloned.1.call-update) | async-done | bytes 16777232 | tf_op jit(solution)/shard_map/all_gather | solution.py:66
  360.9 21.7 %copy.41 = bf16[16,2048,256]{1,2,0:T(8,128)(2,1)} copy(bf16[16,2048,256]{2,1,0:T(8,128)(2,1)} %all-gather.5.cloned.1.call-done) | data formatting | bytes 33554432
  382.6 7.7 %multiply_reduce_fusion = f32[2048,4,64]{0,2,1:T(8,128)S(1)} fusion(bf16[2048,4,16,64]{0,3,1,2:T(8,128)(2,1)} %bitcast.68, f32[2048,4,16]{0,1,2:T(4,128)S(1)} %copy.43), kind=kLoop, calls=%fused_computation.1 | loop fusion | flops 24641536 | bytes 19398656 | tf_op jit(solution)/shard_map/jfh,jfhd->fhd/dot_general | solution.py:78
  390.5 3.3 convolution_convert_fusion
  393.8 93.4 %all-reduce.5.cloned.1.call-done = bf16[2048,1024]{1,0:T(8,128)(2,1)} async-done(((bf16[2048,1024]{1,0:T(8,128)(2,1)}), bf16[2048,1024]{1,0:T(8,128)(2,1)}) %all-reduce.5.cloned.1.call-update) | async-done | bytes 4194320 | tf_op jit(solution)/shard_map/psum | solution.py:87
  487.2 5.8 %multiply_reduce_fusion.2 = (f32[2048]{0:T(1024)S(1)}, f32[2048,1024]{1,0:T(8,128)S(1)}) fusion(bf16[2048,1024]{1,0:T(8,128)(2,1)} %all-reduce.5.cloned.1.call-done, bf16[2048,1024]{1,0:T(8,128)(2,1)} %gather_fusion, bf16[2048,1024]{1,0:T(8,128)(2,1)} %all-reduce.3.cloned.1.call-done), kind=kLoop, calls=%fused_computation.5 | loop fusion | flops 14678016 | bytes 20979712 | tf_op jit(solution)/shard_map/reduce_sum | solution.py:16
  493.0 3.2 copy-done.4
  496.2 6.7 %fusion.14 = f32[2048,1024]{1,0:T(8,128)} fusion(bf16[1,2,1024,1024]{3,2,1,0:T(8,128)(2,1)S(1)} %copy-done.7, f32[2048,1024]{1,0:T(8,128)S(1)} %get-tuple-element.6, f32[1024]{0:T(1024)S(1)} %bitcast.73, f32[2048]{0:T(1024)S(1)} %add_rsqrt_fusion), kind=kOutput, calls=%fused_computation.21 | convolution fusion | flops 4301258752 | bytes 18886656 | tf_op jit(solution)/shard_map/dot_general | solution.py:20
  503.0 15.1 %convolution_convert_fusion.1 = bf16[2048,1024]{1,0:T(8,128)(2,1)} fusion(f32[2048,1024]{1,0:T(8,128)} %fusion.14, bf16[1,1024,1024]{2,1,0:T(8,128)(2,1)} %param.16, bf16[1,2,1024,1024]{3,2,1,0:T(8,128)(2,1)} %param.15, f32[2048,1024]{1,0:T(8,128)} %copy-done.4, f32[1024]{0:T(1024)S(1)} %bitcast.74, f32[2048]{0:T(1024)S(1)} %add_rsqrt_fusion), kind=kOutput, calls=%fused_computation.15 | convolution fusion | flops 8610906112 | bytes 25178112 | tf_op jit(solution)/shard_map/dot_general | solution.py:90
  518.1 47.0 %reduce-scatter.2.cloned.1.call-done = bf16[2048,256]{1,0:T(8,128)(2,1)} async-done(((bf16[2048,1024]{1,0:T(8,128)(2,1)}), bf16[2048,256]{1,0:T(8,128)(2,1)}) %reduce-scatter.2.cloned.1.call-update) | async-done | bytes 1048592 | tf_op jit(solution)/shard_map/reduce_scatter | solution.py:91
  565.2 3.4 add_bitcast_fusion
  (35 shorter events, 0.7 us)
Async XLA Ops:
  6.5 57.1 %copy-start = (bf16[1,1024,1024]{2,1,0:T(8,128)(2,1)S(1)}, bf16[1,1024,1024]{2,1,0:T(8,128)(2,1)}, u32[]{:S(2)}) copy-start(bf16[1,1024,1024]{2,1,0:T(8,128)(2,1)} %param.11) | copy-start | bytes 6291460
  6.5 156.5 %all-reduce.3.cloned.1.call-start = ((), (), s32[]{:S(2)}) async-start(), calls=%async_computation.2 | async-start | bytes 8388608 | tf_op jit(solution)/shard_map/psum | solution.py:53
  69.6 0.7 copy-start.9
  69.6 2.6 copy-start.6
  69.6 197.2 %all-gather.3.cloned.1.call-start = ((), (), s32[]{:S(2)}) async-start(), calls=%async_computation.3 | async-start | bytes 17825792 | tf_op jit(solution)/shard_map/all_gather | solution.py:65
  70.3 3.4 collective-permute-start
  73.7 94.4 %copy-start.8 = (bf16[1,3,1024,256]{3,2,1,0:T(8,128)(2,1)S(1)}, bf16[1,3,1024,256]{3,2,1,0:T(8,128)(2,1)}, u32[]{:S(2)}) copy-start(bf16[1,3,1024,256]{3,2,1,0:T(8,128)(2,1)} %param.13) | copy-start | bytes 4718596
  163.1 5.1 copy-start.2
  163.1 5.9 %copy-start.3 = (bf16[2048,1024]{1,0:T(8,128)(2,1)S(1)}, bf16[2048,1024]{1,0:T(8,128)(2,1)}, u32[]{:S(2)}) copy-start(bf16[2048,1024]{1,0:T(8,128)(2,1)} %all-reduce.3.cloned.1.call-done) | copy-start | bytes 12582916
  174.8 186.0 %all-gather.5.cloned.1.call-start = ((), (), s32[]{:S(2)}) async-start(), calls=%async_computation.4 | async-start | bytes 17825792 | tf_op jit(solution)/shard_map/all_gather | solution.py:66
  176.2 310.9 %all-reduce.5.cloned.1.call-start = ((), (), s32[]{:S(2)}) async-start(), calls=%async_computation.5 | async-start | bytes 8388608 | tf_op jit(solution)/shard_map/psum | solution.py:87
  382.6 7.9 %copy-start.5 = (bf16[1,256,1024]{2,1,0:T(8,128)(2,1)S(1)}, bf16[1,256,1024]{2,1,0:T(8,128)(2,1)}, u32[]{:S(2)}) copy-start(bf16[1,256,1024]{2,1,0:T(8,128)(2,1)} %param.14) | copy-start | bytes 1572868
  393.7 171.4 %reduce-scatter.2.cloned.1.call-start = ((), (), s32[]{:S(2)}) async-start(), calls=%async_computation.6 | async-start | bytes 5242880 | tf_op jit(solution)/shard_map/reduce_scatter | solution.py:91
  487.2 9.1 %copy-start.7 = (bf16[1,2,1024,1024]{3,2,1,0:T(8,128)(2,1)S(1)}, bf16[1,2,1024,1024]{3,2,1,0:T(8,128)(2,1)}, u32[]{:S(2)}) copy-start(bf16[1,2,1024,1024]{3,2,1,0:T(8,128)(2,1)} %param.15) | copy-start | bytes 12582916
  493.0 3.2 copy-start.4
  518.1 50.5 %copy-start.1 = (bf16[1,1024,1024]{2,1,0:T(8,128)(2,1)S(1)}, bf16[1,1024,1024]{2,1,0:T(8,128)(2,1)}, u32[]{:S(2)}) copy-start(bf16[1,1024,1024]{2,1,0:T(8,128)(2,1)} %param.11) | copy-start | bytes 6291460
Sparse Core Ops, SparseCore 0:
  69.7 93.2 all-reduce.2
  175.0 91.8 all-gather.2
  268.5 92.3 all-gather.4
  393.9 93.2 all-reduce.4
  518.2 46.8 reduce-scatter.1
